TPU v7x, 512 devices: a whole 4x4x16 slice. The times are simulated.
512 devices in a mesh: tiles: 128 (over y, z, core), samp: 4 (over x).
Axes of the slice: x: 4, y: 4, z: 16, core: 2. Of those that a mesh axis runs over, the one named last changes fastest.
Arguments:
- samples: bfloat16 [256, 131072], P('samp', 'tiles'), may hold values from -6 to 6
- omega: float32 [1280, 512, 512], P('tiles', 'samp'), may hold values from -1 to 2, as said below
- coords: int32 [1280, 2], P('tiles'), may hold values from 0 to 255, as said below
Outputs:
- updated: float32 [1280, 512, 512], P('tiles', 'samp')
Inputs may be any that keep to these rules, and one draw needn't show every extreme that they name: `coords`: tile k lies with index k // 10 of tiles. Write d for that index, and blocks d * 2 to (d + 1) * 2 - 1 as its own blocks; indices of devices wrap around. The first 2 tiles of d are the diagonal tiles (I, I) of its own blocks in order. Each other tile of d is (I, J) with I an own block and J a block of d + 1, or I a block of d - 1 and J a block of d + 1, or I < J both own blocks. No unordered pair of blocks appears twice in the whole list. `omega`: tiles with I == J are symmetric with diagonal entries from 0.5 to 2.
All inputs are finite; a program needn't handle non-finite values.
Results may differ from a plain program's by a relative error of at most 0.0023.
Values may be sent and summed in bfloat16 or wider, within the bound.
No kernel may reach another device: no remote copies, remote signals or barrier semaphores. Data moves between devices by JAX's collectives and lax.ppermute only.
A program may use at most 64 MiB of HBM per device.

v0:
```python
import jax
import jax.numpy as jnp
from jax import lax
from jax.sharding import PartitionSpec as P

BLK_DEV = 2
ITERS = 2
step_size = 0.25
penalty = 0.2


def with_halo(shard, sides, width):
    for axis, dim in sides:
        size, length = (lax.axis_size(axis), shard.shape[dim])
        up = [(i, (i + 1) % size) for i in range(size)]
        down = [(j, i) for i, j in up]
        last = lax.slice_in_dim(shard, length - width, length, axis=dim)
        leading = lax.slice_in_dim(shard, 0, width, axis=dim)
        before = lax.ppermute(last, axis, up)
        after = lax.ppermute(leading, axis, down)
        shard = jnp.concatenate([before, shard, after], axis=dim)
    return shard


def columns(matrix, start, count):
    return lax.dynamic_slice_in_dim(matrix, start, count, 1)


def add_columns(totals, block, start):
    current = lax.dynamic_slice_in_dim(totals, start, block.shape[1], 1)
    return lax.dynamic_update_slice_in_dim(totals, current + block, start, 1)


def shards(samples, omega, coords):
    quarter = lax.axis_index("samp")
    tile_rows = omega.shape[1]
    width = omega.shape[2]
    own_width = samples.shape[1]
    blocks_all = BLK_DEV * lax.axis_size("tiles")
    first_block = (lax.axis_index("tiles") - 1) * BLK_DEV
    local = (coords - first_block + blocks_all) % blocks_all
    off_diagonal = (coords[:, 0] != coords[:, 1]).astype(jnp.float32)
    offset = quarter * tile_rows
    full_rows = lax.all_gather(samples, "samp", axis=0, tiled=True)
    sample_win = with_halo(full_rows, (("tiles", 1),), own_width)
    count = sample_win.shape[0]
    row_ids = offset + lax.broadcasted_iota(jnp.int32, (tile_rows, width), 0)
    col_ids = lax.broadcasted_iota(jnp.int32, (tile_rows, width), 1)
    diagonal_cells = row_ids == col_ids
    contract_cols = (((1,), (1,)), ((), ()))
    contract_rows = (((0,), (0,)), ((), ()))
    for iteration in range(ITERS):
        omega_low = omega.astype(jnp.bfloat16)
        totals = jnp.zeros((count, 3 * own_width), jnp.float32)
        for tile_slot in range(omega.shape[0]):
            row_start = local[tile_slot, 0] * width
            col_start = local[tile_slot, 1] * width
            rows_low = omega_low[tile_slot]
            row_part = columns(sample_win, row_start + offset, tile_rows)
            col_block = columns(sample_win, col_start, width)
            to_col = jnp.dot(row_part, rows_low, preferred_element_type=jnp.float32)
            to_row = lax.dot_general(
                col_block, rows_low, contract_cols, preferred_element_type=jnp.float32
            )
            totals = add_columns(totals, to_col, col_start)
            totals = add_columns(totals, to_row * off_diagonal[tile_slot], row_start + offset)
        returned = with_halo(totals, (("tiles", 1),), own_width)
        partial_value = (
            totals[:, own_width : 2 * own_width]
            + returned[:, :own_width]
            + returned[:, 4 * own_width :]
        )
        summed = lax.psum(partial_value, "samp")
        product_own = summed.astype(jnp.bfloat16)
        product_win = with_halo(product_own, (("tiles", 1),), own_width)
        new_tiles = []
        for tile_slot in range(omega.shape[0]):
            row_start = local[tile_slot, 0] * width
            col_start = local[tile_slot, 1] * width
            product_rows = columns(product_win, row_start + offset, tile_rows)
            sample_rows = columns(sample_win, row_start + offset, tile_rows)
            sample_cols = columns(sample_win, col_start, width)
            product_cols = columns(product_win, col_start, width)
            first = lax.dot_general(
                product_rows, sample_cols, contract_rows, preferred_element_type=jnp.float32
            )
            second = lax.dot_general(
                sample_rows, product_cols, contract_rows, preferred_element_type=jnp.float32
            )
            grad = (first + second) / (2.0 * count)
            value = omega[tile_slot] - step_size * grad
            shrunk = jnp.sign(value) * jnp.maximum(jnp.abs(value) - step_size * penalty, 0.0)
            positive = 0.5 * (value + jnp.sqrt(value * value + 4.0 * step_size))
            same_block = coords[tile_slot, 0] == coords[tile_slot, 1]
            new_tiles.append(jnp.where(diagonal_cells & same_block, positive, shrunk))
        omega = jnp.stack(new_tiles)
    return omega


def solution(mesh):
    in_specs = (P("samp", "tiles"), P("tiles", "samp", None), P("tiles", None))
    out_specs = P("tiles", "samp", None)
    return jax.shard_map(shards, mesh=mesh, in_specs=in_specs, out_specs=out_specs, check_vma=False)
```

profile of v0, /device:TPU:4, one launch (start us, length us, event | category | flops | bytes accessed | tf_op | source)
XLA Modules:
  0.0 228.5 jit_solution(8097895202772696019)
XLA Ops:
  0.0 16.8 %all_gather.3 = bf16[256,1024]{1,0:T(8,128)(2,1)S(1)} all-gather(bf16[64,1024]{1,0:T(8,128)(2,1)} %param.3), channel_id=1, replica_groups=mesh['tiles'=128,'samp'=4] {'samp'}, dimensions={0}, use_global_device_ids=true | all-gather | bytes 655360 | tf_op jit(solution)/shard_map/all_gather | solution.py:44
  16.8 1.9 collective-permute-start
  18.7 7.0 %collective-permute-start.1 = (bf16[256,1024]{1,0:T(8,128)(2,1)S(1)}, bf16[256,1024]{1,0:T(8,128)(2,1)}, u32[]{:S(2)}, u32[]{:S(2)}) collective-permute-start(bf16[256,1024]{1,0:T(8,128)(2,1)S(1)} %all_gather.3), channel_id=1, source_target_pairs={{4,0},{8,4},{12,8},{16,12},{20,16},{24,20},{28,24},{32,28},{36,32}... | collective-permute-start | bytes 1572872 | tf_op jit(solution)/shard_map/ppermute | solution.py:20
  40.3 1.9 convert_element_type.14
  43.1 1.1 constant_dynamic-update-slice_fusion.2
  44.2 1.1 constant_dynamic-update-slice_fusion
  56.7 1.9 collective-permute-start.2
  58.6 7.0 %collective-permute-start.3 = (f32[256,1024]{1,0:T(8,128)S(1)}, f32[256,1024]{1,0:T(8,128)S(1)}, u32[]{:S(2)}, u32[]{:S(2)}) collective-permute-start(f32[256,1024]{1,0:T(8,128)S(1)} %get-tuple-element.8), channel_id=1, source_target_pairs={{4,0},{8,4},{12,8},{16,12},{20,16},{24,20},{28,24},{32,28},{36,32}... | collective-permute-start | bytes 3145736 | tf_op jit(solution)/shard_map/ppermute | solution.py:20
  65.6 10.5 %collective-permute-done.2 = f32[256,1024]{1,0:T(8,128)S(1)} collective-permute-done((f32[256,1024]{1,0:T(8,128)S(1)}, f32[256,1024]{1,0:T(8,128)S(1)}, u32[]{:S(2)}, u32[]{:S(2)}) %collective-permute-start.2) | collective-permute-done | bytes 1048608 | tf_op jit(solution)/shard_map/ppermute | solution.py:19
  76.1 1.8 collective-permute-done.3
  78.2 28.7 %all-reduce.2 = bf16[256,1024]{1,0:T(8,128)(2,1)S(1)} all-reduce(f32[256,1024]{1,0:T(8,128)S(1)} %fusion.61), channel_id=1, replica_groups=mesh['tiles'=128,'samp'=4] {'samp'}, use_global_device_ids=true, to_apply=%region_0.1 | all-reduce | flops 262144 | bytes 1572864 | tf_op jit(solution)/shard_map/psum | solution.py:73
  106.9 1.9 collective-permute-start.4
  108.8 7.1 %collective-permute-start.5 = (bf16[256,1024]{1,0:T(8,128)(2,1)S(1)}, bf16[256,1024]{1,0:T(8,128)(2,1)S(1)}, u32[]{:S(2)}, u32[]{:S(2)}) collective-permute-start(bf16[256,1024]{1,0:T(8,128)(2,1)S(1)} %all-reduce.2), channel_id=1, source_target_pairs={{4,0},{8,4},{12,8},{16,12},{20,16},{24,20},{28,24},{32,28},{36,32}... | collective-permute-start | bytes 1572872 | tf_op jit(solution)/shard_map/ppermute | solution.py:20
  149.9 1.9 collective-permute-start.6
  151.9 7.0 %collective-permute-start.7 = (f32[256,1024]{1,0:T(8,128)S(1)}, f32[256,1024]{1,0:T(8,128)S(1)}, u32[]{:S(2)}, u32[]{:S(2)}) collective-permute-start(f32[256,1024]{1,0:T(8,128)S(1)} %get-tuple-element.6), channel_id=1, source_target_pairs={{4,0},{8,4},{12,8},{16,12},{20,16},{24,20},{28,24},{32,28},{36,32}... | collective-permute-start | bytes 3145736 | tf_op jit(solution)/shard_map/ppermute | solution.py:20
  158.8 10.5 %collective-permute-done.6 = f32[256,1024]{1,0:T(8,128)S(1)} collective-permute-done((f32[256,1024]{1,0:T(8,128)S(1)}, f32[256,1024]{1,0:T(8,128)S(1)}, u32[]{:S(2)}, u32[]{:S(2)}) %collective-permute-start.6) | collective-permute-done | bytes 1048608 | tf_op jit(solution)/shard_map/ppermute | solution.py:19
  169.4 1.8 collective-permute-done.7
  171.4 31.7 %all-reduce.3 = bf16[256,1024]{1,0:T(8,128)(2,1)S(1)} all-reduce(f32[256,1024]{1,0:T(8,128)S(1)} %fusion.60), channel_id=1, replica_groups=mesh['tiles'=128,'samp'=4] {'samp'}, use_global_device_ids=true, to_apply=%region_1.2 | all-reduce | flops 262144 | bytes 1572864 | tf_op jit(solution)/shard_map/psum | solution.py:73
  203.1 1.9 collective-permute-start.8
  205.1 7.2 %collective-permute-start.9 = (bf16[256,1024]{1,0:T(8,128)(2,1)S(1)}, bf16[256,1024]{1,0:T(8,128)(2,1)S(1)}, u32[]{:S(2)}, u32[]{:S(2)}) collective-permute-start(bf16[256,1024]{1,0:T(8,128)(2,1)S(1)} %all-reduce.3), channel_id=1, source_target_pairs={{4,0},{8,4},{12,8},{16,12},{20,16},{24,20},{28,24},{32,28},{36,32}... | collective-permute-start | bytes 1572872 | tf_op jit(solution)/shard_map/ppermute | solution.py:20
  212.2 4.7 %collective-permute-done.8 = bf16[256,1024]{1,0:T(8,128)(2,1)S(1)} collective-permute-done((bf16[256,1024]{1,0:T(8,128)(2,1)S(1)}, bf16[256,1024]{1,0:T(8,128)(2,1)S(1)}, u32[]{:S(2)}, u32[]{:S(2)}) %collective-permute-start.8) | collective-permute-done | bytes 524320 | tf_op jit(solution)/shard_map/ppermute | solution.py:19
  216.9 1.8 collective-permute-done.9
  225.8 1.5 copy-done.20
  227.3 1.2 bitcast_dynamic-update-slice_fusion
  (141 shorter events, 42.4 us)
Async XLA Ops:
  16.8 26.3 %collective-permute-start = (bf16[256,1024]{1,0:T(8,128)(2,1)S(1)}, bf16[256,1024]{1,0:T(8,128)(2,1)}, u32[]{:S(2)}, u32[]{:S(2)}) collective-permute-start(bf16[256,1024]{1,0:T(8,128)(2,1)S(1)} %all_gather.3), channel_id=1, source_target_pairs={{0,4},{4,8},{8,12},{12,16},{16,20},{20,24},{24,28},{28,32},{32,36}... | collective-permute-start | bytes 1572872 | tf_op jit(solution)/shard_map/ppermute | solution.py:19
  18.7 25.5 %collective-permute-start.1 = (bf16[256,1024]{1,0:T(8,128)(2,1)S(1)}, bf16[256,1024]{1,0:T(8,128)(2,1)}, u32[]{:S(2)}, u32[]{:S(2)}) collective-permute-start(bf16[256,1024]{1,0:T(8,128)(2,1)S(1)} %all_gather.3), channel_id=1, source_target_pairs={{4,0},{8,4},{12,8},{16,12},{20,16},{24,20},{28,24},{32,28},{36,32}... | collective-permute-start | bytes 1572872 | tf_op jit(solution)/shard_map/ppermute | solution.py:20
  40.3 2.1 copy-start.19
  56.7 19.4 %collective-permute-start.2 = (f32[256,1024]{1,0:T(8,128)S(1)}, f32[256,1024]{1,0:T(8,128)S(1)}, u32[]{:S(2)}, u32[]{:S(2)}) collective-permute-start(f32[256,1024]{1,0:T(8,128)S(1)} %get-tuple-element.7), channel_id=1, source_target_pairs={{0,4},{4,8},{8,12},{12,16},{16,20},{20,24},{24,28},{28,32},{32,36}... | collective-permute-start | bytes 3145736 | tf_op jit(solution)/shard_map/ppermute | solution.py:19
  58.6 19.3 %collective-permute-start.3 = (f32[256,1024]{1,0:T(8,128)S(1)}, f32[256,1024]{1,0:T(8,128)S(1)}, u32[]{:S(2)}, u32[]{:S(2)}) collective-permute-start(f32[256,1024]{1,0:T(8,128)S(1)} %get-tuple-element.8), channel_id=1, source_target_pairs={{4,0},{8,4},{12,8},{16,12},{20,16},{24,20},{28,24},{32,28},{36,32}... | collective-permute-start | bytes 3145736 | tf_op jit(solution)/shard_map/ppermute | solution.py:20
  106.9 22.9 %collective-permute-start.4 = (bf16[256,1024]{1,0:T(8,128)(2,1)S(1)}, bf16[256,1024]{1,0:T(8,128)(2,1)S(1)}, u32[]{:S(2)}, u32[]{:S(2)}) collective-permute-start(bf16[256,1024]{1,0:T(8,128)(2,1)S(1)} %all-reduce.2), channel_id=1, source_target_pairs={{0,4},{4,8},{8,12},{12,16},{16,20},{20,24},{24,28},{28,32},{32,36}... | collective-permute-start | bytes 1572872 | tf_op jit(solution)/shard_map/ppermute | solution.py:19
  108.8 21.0 %collective-permute-start.5 = (bf16[256,1024]{1,0:T(8,128)(2,1)S(1)}, bf16[256,1024]{1,0:T(8,128)(2,1)S(1)}, u32[]{:S(2)}, u32[]{:S(2)}) collective-permute-start(bf16[256,1024]{1,0:T(8,128)(2,1)S(1)} %all-reduce.2), channel_id=1, source_target_pairs={{4,0},{8,4},{12,8},{16,12},{20,16},{24,20},{28,24},{32,28},{36,32}... | collective-permute-start | bytes 1572872 | tf_op jit(solution)/shard_map/ppermute | solution.py:20
  131.1 1.7 copy-start
  135.2 1.6 copy-start.3
  136.9 1.5 copy-start.5
  138.4 1.7 copy-start.7
  140.1 1.5 copy-start.9
  141.6 1.7 copy-start.11
  143.3 1.6 copy-start.13
  144.9 1.5 copy-start.15
  146.5 1.6 copy-start.17
  149.9 19.4 %collective-permute-start.6 = (f32[256,1024]{1,0:T(8,128)S(1)}, f32[256,1024]{1,0:T(8,128)S(1)}, u32[]{:S(2)}, u32[]{:S(2)}) collective-permute-start(f32[256,1024]{1,0:T(8,128)S(1)} %get-tuple-element.5), channel_id=1, source_target_pairs={{0,4},{4,8},{8,12},{12,16},{16,20},{20,24},{24,28},{28,32},{32,36}... | collective-permute-start | bytes 3145736 | tf_op jit(solution)/shard_map/ppermute | solution.py:19
  151.9 19.3 %collective-permute-start.7 = (f32[256,1024]{1,0:T(8,128)S(1)}, f32[256,1024]{1,0:T(8,128)S(1)}, u32[]{:S(2)}, u32[]{:S(2)}) collective-permute-start(f32[256,1024]{1,0:T(8,128)S(1)} %get-tuple-element.6), channel_id=1, source_target_pairs={{4,0},{8,4},{12,8},{16,12},{20,16},{24,20},{28,24},{32,28},{36,32}... | collective-permute-start | bytes 3145736 | tf_op jit(solution)/shard_map/ppermute | solution.py:20
  203.1 13.8 %collective-permute-start.8 = (bf16[256,1024]{1,0:T(8,128)(2,1)S(1)}, bf16[256,1024]{1,0:T(8,128)(2,1)S(1)}, u32[]{:S(2)}, u32[]{:S(2)}) collective-permute-start(bf16[256,1024]{1,0:T(8,128)(2,1)S(1)} %all-reduce.3), channel_id=1, source_target_pairs={{0,4},{4,8},{8,12},{12,16},{16,20},{20,24},{24,28},{28,32},{32,36}... | collective-permute-start | bytes 1572872 | tf_op jit(solution)/shard_map/ppermute | solution.py:19
  205.1 13.6 %collective-permute-start.9 = (bf16[256,1024]{1,0:T(8,128)(2,1)S(1)}, bf16[256,1024]{1,0:T(8,128)(2,1)S(1)}, u32[]{:S(2)}, u32[]{:S(2)}) collective-permute-start(bf16[256,1024]{1,0:T(8,128)(2,1)S(1)} %all-reduce.3), channel_id=1, source_target_pairs={{4,0},{8,4},{12,8},{16,12},{20,16},{24,20},{28,24},{32,28},{36,32}... | collective-permute-start | bytes 1572872 | tf_op jit(solution)/shard_map/ppermute | solution.py:20
  220.4 1.2 copy-start.4
  220.9 1.3 copy-start.6
  224.8 2.5 %copy-start.2 = (f32[128,512]{1,0:T(8,128)S(1)}, f32[128,512]{1,0:T(8,128)}, u32[]{:S(2)}) copy-start(f32[128,512]{1,0:T(8,128)} %copy-done.1) | copy-start | bytes 786436
  225.8 1.5 copy-start.20
  (7 other events, 6.9 us)
where the time goes:
time: 230 us; the launch traced here: 228 us
  blocking collectives  77.2 us (34%)
  starting transfers between devices  44.8 us (19%)
  matrix products  36.4 us (16%)
  waiting for transfers between devices  31.1 us (14%)
  between operations  26.3 us (11%)
  local copies, waits for them, and re-layouts  9.34 us (4%)
  other arithmetic  3.42 us (1%)
    psum x2, blocking collectives, shards(): summed = lax.psum(partial_value, 'samp')  60.4 us
    ppermute x5, starting transfers between devices, with_halo(): after = lax.ppermute(leading, axis, down)  35.2 us
    ppermute x5, waiting for transfers between devices, with_halo(): before = lax.ppermute(last, axis, up)  25.8 us
    dot_general x20, matrix products, shards(): lax.dot_general(col_block, rows_low, contract_cols, preferred_element_typ...  17 us
    all_gather x1, blocking collectives, shards(): full_rows = lax.all_gather(samples, 'samp', axis=0, tiled=True)  16.8 us
    dot_general x20, matrix products, shards(): lax.dot_general(product_rows, sample_cols, contract_rows, preferred_eleme...  10.6 us
    ppermute x5, starting transfers between devices, with_halo(): before = lax.ppermute(last, axis, up)  9.59 us
    ppermute x5, waiting for transfers between devices, with_halo(): after = lax.ppermute(leading, axis, down)  5.27 us
  transfers between devices with their start and end apart: 10, of which 6 were waited for; matrix products, arithmetic and copies ran while one was open for 3% of the time, Pallas kernels for 0%

commit v1 on v0

--- a/solution.py
+++ b/solution.py
@@ -7,6 +7,14 @@
 ITERS = 2
 step_size = 0.25
 penalty = 0.2
+
+
+def sum_by_hops(block, axis):
+    size, acc = (lax.axis_size(axis), block)
+    for stride in [1 << k for k in range(size.bit_length() - 1)]:
+        swap = [(i, i ^ stride) for i in range(size)]
+        acc = acc + lax.ppermute(acc, axis, swap)
+    return acc
 
 
 def with_halo(shard, sides, width):
@@ -70,7 +78,7 @@
             + returned[:, :own_width]
             + returned[:, 4 * own_width :]
         )
-        summed = lax.psum(partial_value, "samp")
+        summed = sum_by_hops(partial_value, "samp")
         product_own = summed.astype(jnp.bfloat16)
         product_win = with_halo(product_own, (("tiles", 1),), own_width)
         new_tiles = []

time: 230 us -> 266 us (1.16)
  the two profiles are of different devices: /device:TPU:4 before, /device:TPU:30 now
where the time goes in v1:
time: 266 us; the launch traced here: 265 us
  waiting for transfers between devices  112 us (42%)
  starting transfers between devices  65.4 us (25%)
  matrix products  37.7 us (14%)
  between operations  25.9 us (10%)
  blocking collectives  13.6 us (5%)
  local copies, waits for them, and re-layouts  6.13 us (2%)
  other arithmetic  3.95 us (1%)
    ppermute x4, waiting for transfers between devices, sum_by_hops(): acc = acc + lax.ppermute(acc, axis, swap)  81.2 us
    ppermute x5, starting transfers between devices, with_halo(): after = lax.ppermute(leading, axis, down)  47.6 us
    ppermute x5, waiting for transfers between devices, with_halo(): before = lax.ppermute(last, axis, up)  25.8 us
    dot_general x20, matrix products, shards(): lax.dot_general(col_block, rows_low, contract_cols, preferred_element_typ...  17.4 us
    all_gather x1, blocking collectives, shards(): full_rows = lax.all_gather(samples, 'samp', axis=0, tiled=True)  13.6 us
    dot_general x20, matrix products, shards(): lax.dot_general(product_rows, sample_cols, contract_rows, preferred_eleme...  10 us
    ppermute x5, starting transfers between devices, with_halo(): before = lax.ppermute(last, axis, up)  9.59 us
    ppermute x4, starting transfers between devices, sum_by_hops(): acc = acc + lax.ppermute(acc, axis, swap)  8.24 us
  transfers between devices with their start and end apart: 14, of which 10 were waited for; matrix products, arithmetic and copies ran while one was open for 2% of the time, Pallas kernels for 0%

profile of v1, /device:TPU:30, one launch (start us, length us, event | category | flops | bytes accessed | tf_op | source)
XLA Modules:
  0.0 265.0 jit_solution(7979956825956479500)
XLA Ops:
  0.0 13.6 %all_gather.3 = bf16[256,1024]{1,0:T(8,128)(2,1)S(1)} all-gather(bf16[64,1024]{1,0:T(8,128)(2,1)} %param.3), channel_id=1, replica_groups=mesh['tiles'=128,'samp'=4] {'samp'}, dimensions={0}, use_global_device_ids=true | all-gather | bytes 655360 | tf_op jit(solution)/shard_map/all_gather | solution.py:52
  13.6 1.9 collective-permute-start
  15.5 7.6 %collective-permute-start.1 = (bf16[256,1024]{1,0:T(8,128)(2,1)S(1)}, bf16[256,1024]{1,0:T(8,128)(2,1)S(1)}, u32[]{:S(2)}, u32[]{:S(2)}) collective-permute-start(bf16[256,1024]{1,0:T(8,128)(2,1)S(1)} %all_gather.3), channel_id=1, source_target_pairs={{4,0},{8,4},{12,8},{16,12},{20,16},{24,20},{28,24},{32,28},{36,32}... | collective-permute-start | bytes 1572872 | tf_op jit(solution)/shard_map/ppermute | solution.py:28
  37.7 1.9 convert_element_type.14
  52.6 1.9 collective-permute-start.2
  54.5 6.1 %collective-permute-start.3 = (f32[256,1024]{0,1:T(8,128)S(1)}, f32[256,1024]{0,1:T(8,128)S(1)}, u32[]{:S(2)}, u32[]{:S(2)}) collective-permute-start(f32[256,1024]{0,1:T(8,128)S(1)} %get-tuple-element.8), channel_id=1, source_target_pairs={{4,0},{8,4},{12,8},{16,12},{20,16},{24,20},{28,24},{32,28},{36,32}... | collective-permute-start | bytes 3145736 | tf_op jit(solution)/shard_map/ppermute | solution.py:28
  60.6 10.5 %collective-permute-done.2 = f32[256,1024]{0,1:T(8,128)S(1)} collective-permute-done((f32[256,1024]{0,1:T(8,128)S(1)}, f32[256,1024]{0,1:T(8,128)S(1)}, u32[]{:S(2)}, u32[]{:S(2)}) %collective-permute-start.2) | collective-permute-done | bytes 1048608 | tf_op jit(solution)/shard_map/ppermute | solution.py:27
  71.1 1.8 collective-permute-done.3
  73.1 2.4 collective-permute-start.4
  75.5 22.4 %collective-permute-done.4 = f32[256,1024]{0,1:T(8,128)S(1)} collective-permute-done((f32[256,1024]{0,1:T(8,128)S(1)}, f32[256,1024]{0,1:T(8,128)S(1)}, u32[]{:S(2)}, u32[]{:S(2)}) %collective-permute-start.4) | collective-permute-done | bytes 1048608 | tf_op jit(solution)/shard_map/ppermute | solution.py:16
  98.0 1.9 collective-permute-start.5
  100.0 20.1 %collective-permute-done.5 = f32[256,1024]{0,1:T(8,128)S(1)} collective-permute-done((f32[256,1024]{0,1:T(8,128)S(1)}, f32[256,1024]{0,1:T(8,128)S(1)}, u32[]{:S(2)}, u32[]{:S(2)}) %collective-permute-start.5) | collective-permute-done | bytes 1048608 | tf_op jit(solution)/shard_map/ppermute | solution.py:16
  120.3 1.9 collective-permute-start.6
  122.3 13.8 %collective-permute-start.7 = (bf16[256,1024]{0,1:T(8,128)(2,1)S(1)}, bf16[256,1024]{0,1:T(8,128)(2,1)S(1)}, u32[]{:S(2)}, u32[]{:S(2)}) collective-permute-start(bf16[256,1024]{0,1:T(8,128)(2,1)S(1)} %add_convert_fusion.1), channel_id=1, source_target_pairs={{4,0},{8,4},{12,8},{16,12},{20,16},{24,20},{28,24},{32,28},{36,32}... | collective-permute-start | bytes 1572872 | tf_op jit(solution)/shard_map/ppermute | solution.py:28
  169.6 1.9 collective-permute-start.8
  171.5 5.8 %collective-permute-start.9 = (f32[256,1024]{0,1:T(8,128)S(1)}, f32[256,1024]{0,1:T(8,128)S(1)}, u32[]{:S(2)}, u32[]{:S(2)}) collective-permute-start(f32[256,1024]{0,1:T(8,128)S(1)} %get-tuple-element.6), channel_id=1, source_target_pairs={{4,0},{8,4},{12,8},{16,12},{20,16},{24,20},{28,24},{32,28},{36,32}... | collective-permute-start | bytes 3145736 | tf_op jit(solution)/shard_map/ppermute | solution.py:28
  177.3 10.5 %collective-permute-done.8 = f32[256,1024]{0,1:T(8,128)S(1)} collective-permute-done((f32[256,1024]{0,1:T(8,128)S(1)}, f32[256,1024]{0,1:T(8,128)S(1)}, u32[]{:S(2)}, u32[]{:S(2)}) %collective-permute-start.8) | collective-permute-done | bytes 1048608 | tf_op jit(solution)/shard_map/ppermute | solution.py:27
  189.8 2.0 collective-permute-start.10
  191.8 22.4 %collective-permute-done.10 = f32[256,1024]{0,1:T(8,128)S(1)} collective-permute-done((f32[256,1024]{0,1:T(8,128)S(1)}, f32[256,1024]{0,1:T(8,128)S(1)}, u32[]{:S(2)}, u32[]{:S(2)}) %collective-permute-start.10) | collective-permute-done | bytes 1048608 | tf_op jit(solution)/shard_map/ppermute | solution.py:16
  214.3 1.9 collective-permute-start.11
  216.2 16.3 %collective-permute-done.11 = f32[256,1024]{0,1:T(8,128)S(1)} collective-permute-done((f32[256,1024]{0,1:T(8,128)S(1)}, f32[256,1024]{0,1:T(8,128)S(1)}, u32[]{:S(2)}, u32[]{:S(2)}) %collective-permute-start.11) | collective-permute-done | bytes 1048608 | tf_op jit(solution)/shard_map/ppermute | solution.py:16
  232.7 1.9 collective-permute-start.12
  234.6 14.4 %collective-permute-start.13 = (bf16[256,1024]{0,1:T(8,128)(2,1)S(1)}, bf16[256,1024]{0,1:T(8,128)(2,1)S(1)}, u32[]{:S(2)}, u32[]{:S(2)}) collective-permute-start(bf16[256,1024]{0,1:T(8,128)(2,1)S(1)} %add_convert_fusion), channel_id=1, source_target_pairs={{4,0},{8,4},{12,8},{16,12},{20,16},{24,20},{28,24},{32,28},{36,32}... | collective-permute-start | bytes 1572872 | tf_op jit(solution)/shard_map/ppermute | solution.py:28
  249.1 4.7 %collective-permute-done.12 = bf16[256,1024]{0,1:T(8,128)(2,1)S(1)} collective-permute-done((bf16[256,1024]{0,1:T(8,128)(2,1)S(1)}, bf16[256,1024]{0,1:T(8,128)(2,1)S(1)}, u32[]{:S(2)}, u32[]{:S(2)}) %collective-permute-start.12) | collective-permute-done | bytes 524320 | tf_op jit(solution)/shard_map/ppermute | solution.py:27
  (115 shorter events, 49.4 us)
Async XLA Ops:
  13.6 26.9 %collective-permute-start = (bf16[256,1024]{1,0:T(8,128)(2,1)S(1)}, bf16[256,1024]{1,0:T(8,128)(2,1)S(1)}, u32[]{:S(2)}, u32[]{:S(2)}) collective-permute-start(bf16[256,1024]{1,0:T(8,128)(2,1)S(1)} %all_gather.3), channel_id=1, source_target_pairs={{0,4},{4,8},{8,12},{12,16},{16,20},{20,24},{24,28},{28,32},{32,36}... | collective-permute-start | bytes 1572872 | tf_op jit(solution)/shard_map/ppermute | solution.py:27
  15.5 25.1 %collective-permute-start.1 = (bf16[256,1024]{1,0:T(8,128)(2,1)S(1)}, bf16[256,1024]{1,0:T(8,128)(2,1)S(1)}, u32[]{:S(2)}, u32[]{:S(2)}) collective-permute-start(bf16[256,1024]{1,0:T(8,128)(2,1)S(1)} %all_gather.3), channel_id=1, source_target_pairs={{4,0},{8,4},{12,8},{16,12},{20,16},{24,20},{28,24},{32,28},{36,32}... | collective-permute-start | bytes 1572872 | tf_op jit(solution)/shard_map/ppermute | solution.py:28
  37.7 2.1 copy-start.1
  52.6 18.5 %collective-permute-start.2 = (f32[256,1024]{0,1:T(8,128)S(1)}, f32[256,1024]{0,1:T(8,128)S(1)}, u32[]{:S(2)}, u32[]{:S(2)}) collective-permute-start(f32[256,1024]{0,1:T(8,128)S(1)} %get-tuple-element.7), channel_id=1, source_target_pairs={{0,4},{4,8},{8,12},{12,16},{16,20},{20,24},{24,28},{28,32},{32,36}... | collective-permute-start | bytes 3145736 | tf_op jit(solution)/shard_map/ppermute | solution.py:27
  54.5 18.4 %collective-permute-start.3 = (f32[256,1024]{0,1:T(8,128)S(1)}, f32[256,1024]{0,1:T(8,128)S(1)}, u32[]{:S(2)}, u32[]{:S(2)}) collective-permute-start(f32[256,1024]{0,1:T(8,128)S(1)} %get-tuple-element.8), channel_id=1, source_target_pairs={{4,0},{8,4},{12,8},{16,12},{20,16},{24,20},{28,24},{32,28},{36,32}... | collective-permute-start | bytes 3145736 | tf_op jit(solution)/shard_map/ppermute | solution.py:28
  73.1 24.8 %collective-permute-start.4 = (f32[256,1024]{0,1:T(8,128)S(1)}, f32[256,1024]{0,1:T(8,128)S(1)}, u32[]{:S(2)}, u32[]{:S(2)}) collective-permute-start(f32[256,1024]{0,1:T(8,128)S(1)} %fusion.61), channel_id=1, source_target_pairs={{0,1},{1,0},{2,3},{3,2},{4,5},{5,4},{6,7},{7,6},{8,9},{9,8},{10,11... | collective-permute-start | bytes 3145736 | tf_op jit(solution)/shard_map/ppermute | solution.py:16
  98.0 22.1 %collective-permute-start.5 = (f32[256,1024]{0,1:T(8,128)S(1)}, f32[256,1024]{0,1:T(8,128)S(1)}, u32[]{:S(2)}, u32[]{:S(2)}) collective-permute-start(f32[256,1024]{0,1:T(8,128)S(1)} %add.361), channel_id=1, source_target_pairs={{0,2},{1,3},{2,0},{3,1},{4,6},{5,7},{6,4},{7,5},{8,10},{9,11},{10,... | collective-permute-start | bytes 3145736 | tf_op jit(solution)/shard_map/ppermute | solution.py:16
  120.3 29.5 %collective-permute-start.6 = (bf16[256,1024]{0,1:T(8,128)(2,1)S(1)}, bf16[256,1024]{0,1:T(8,128)(2,1)S(1)}, u32[]{:S(2)}, u32[]{:S(2)}) collective-permute-start(bf16[256,1024]{0,1:T(8,128)(2,1)S(1)} %add_convert_fusion.1), channel_id=1, source_target_pairs={{0,4},{4,8},{8,12},{12,16},{16,20},{20,24},{24,28},{28,32},{32,36}... | collective-permute-start | bytes 1572872 | tf_op jit(solution)/shard_map/ppermute | solution.py:27
  122.3 27.6 %collective-permute-start.7 = (bf16[256,1024]{0,1:T(8,128)(2,1)S(1)}, bf16[256,1024]{0,1:T(8,128)(2,1)S(1)}, u32[]{:S(2)}, u32[]{:S(2)}) collective-permute-start(bf16[256,1024]{0,1:T(8,128)(2,1)S(1)} %add_convert_fusion.1), channel_id=1, source_target_pairs={{4,0},{8,4},{12,8},{16,12},{20,16},{24,20},{28,24},{32,28},{36,32}... | collective-permute-start | bytes 1572872 | tf_op jit(solution)/shard_map/ppermute | solution.py:28
  151.1 1.7 copy-start
  169.6 18.2 %collective-permute-start.8 = (f32[256,1024]{0,1:T(8,128)S(1)}, f32[256,1024]{0,1:T(8,128)S(1)}, u32[]{:S(2)}, u32[]{:S(2)}) collective-permute-start(f32[256,1024]{0,1:T(8,128)S(1)} %get-tuple-element.5), channel_id=1, source_target_pairs={{0,4},{4,8},{8,12},{12,16},{16,20},{20,24},{24,28},{28,32},{32,36}... | collective-permute-start | bytes 3145736 | tf_op jit(solution)/shard_map/ppermute | solution.py:27
  171.5 18.1 %collective-permute-start.9 = (f32[256,1024]{0,1:T(8,128)S(1)}, f32[256,1024]{0,1:T(8,128)S(1)}, u32[]{:S(2)}, u32[]{:S(2)}) collective-permute-start(f32[256,1024]{0,1:T(8,128)S(1)} %get-tuple-element.6), channel_id=1, source_target_pairs={{4,0},{8,4},{12,8},{16,12},{20,16},{24,20},{28,24},{32,28},{36,32}... | collective-permute-start | bytes 3145736 | tf_op jit(solution)/shard_map/ppermute | solution.py:28
  189.8 24.3 %collective-permute-start.10 = (f32[256,1024]{0,1:T(8,128)S(1)}, f32[256,1024]{0,1:T(8,128)S(1)}, u32[]{:S(2)}, u32[]{:S(2)}) collective-permute-start(f32[256,1024]{0,1:T(8,128)S(1)} %fusion.60), channel_id=1, source_target_pairs={{0,1},{1,0},{2,3},{3,2},{4,5},{5,4},{6,7},{7,6},{8,9},{9,8},{10,11... | collective-permute-start | bytes 3145736 | tf_op jit(solution)/shard_map/ppermute | solution.py:16
  214.3 18.2 %collective-permute-start.11 = (f32[256,1024]{0,1:T(8,128)S(1)}, f32[256,1024]{0,1:T(8,128)S(1)}, u32[]{:S(2)}, u32[]{:S(2)}) collective-permute-start(f32[256,1024]{0,1:T(8,128)S(1)} %add.801), channel_id=1, source_target_pairs={{0,2},{1,3},{2,0},{3,1},{4,6},{5,7},{6,4},{7,5},{8,10},{9,11},{10,... | collective-permute-start | bytes 3145736 | tf_op jit(solution)/shard_map/ppermute | solution.py:16
  232.7 21.1 %collective-permute-start.12 = (bf16[256,1024]{0,1:T(8,128)(2,1)S(1)}, bf16[256,1024]{0,1:T(8,128)(2,1)S(1)}, u32[]{:S(2)}, u32[]{:S(2)}) collective-permute-start(bf16[256,1024]{0,1:T(8,128)(2,1)S(1)} %add_convert_fusion), channel_id=1, source_target_pairs={{0,4},{4,8},{8,12},{12,16},{16,20},{20,24},{24,28},{28,32},{32,36}... | collective-permute-start | bytes 1572872 | tf_op jit(solution)/shard_map/ppermute | solution.py:27
  234.6 20.9 %collective-permute-start.13 = (bf16[256,1024]{0,1:T(8,128)(2,1)S(1)}, bf16[256,1024]{0,1:T(8,128)(2,1)S(1)}, u32[]{:S(2)}, u32[]{:S(2)}) collective-permute-start(bf16[256,1024]{0,1:T(8,128)(2,1)S(1)} %add_convert_fusion), channel_id=1, source_target_pairs={{4,0},{8,4},{12,8},{16,12},{20,16},{24,20},{28,24},{32,28},{36,32}... | collective-permute-start | bytes 1572872 | tf_op jit(solution)/shard_map/ppermute | solution.py:28
  262.3 1.5 copy-start.2
